TPU v7x, 256 devices: a whole 4x4x8 slice. The times are simulated.
256 devices in a mesh: seq: 32 (over x, y, core), exp: 8 (over z).
Axes of the slice: x: 4, y: 4, z: 8, core: 2. Of those that a mesh axis runs over, the one named last changes fastest.
Arguments:
- tokens: bfloat16 [96, 4, 1024], P('exp'), may hold values from -48 to 48
- attn_gain: float32 [1024], replicated, may hold values from 0.1 to 1.9
- w_qkv: bfloat16 [3072, 1024], P('seq'), may hold values from -0.1875 to 0.1875
- window_cache: bfloat16 [2, 96, 4096, 1024], P(None, 'exp', 'seq'), may hold values from -180 to 180
- sink_cache: bfloat16 [2, 96, 4, 1024], P(None, 'exp'), may hold values from -6 to 6
- lengths: int32 [96], P('exp'), may hold values from 8 to 16384, as said below
- w_out: bfloat16 [1024, 1024], P('seq'), may hold values from -0.1875 to 0.1875
- moe_gain: float32 [1024], replicated, may hold values from 0.1 to 1.9
- router: bfloat16 [1024, 16], replicated, may hold values from -0.1875 to 0.1875
- expert_ids: int32 [96, 4, 2], P('exp'), may hold values from 0 to 15, all different within a row
- slot_order: int32 [8, 48], P('exp'), may hold values from 0 to 47, each once within a row
- expert_in: bfloat16 [2, 8, 5632, 1024], P(None, 'exp', 'seq'), may hold values from -0.1875 to 0.1875
- expert_down: bfloat16 [8, 5632, 1024], P('exp', 'seq'), may hold values from -0.109375 to 0.109375
Outputs:
- output: bfloat16 [96, 4, 1024], P('exp')
Inputs may be any that keep to these rules, and one draw needn't show every extreme that they name: `lengths`: at least one request holds 16384 tokens. `expert_ids`: the 2 experts of a token differ, and every expert is named by some token. `slot_order`: each group's row holds every number of 0 to 47 once.
All inputs are finite; a program needn't handle non-finite values.
Results may differ from a plain program's by a relative error of at most 0.0083.
The roundings to bfloat16 on the way count: a program that leaves them out, or rounds other values in their place, can miss the bound.
Values may be sent and summed in bfloat16 or wider, within the bound.
A program may use at most 64 MiB of HBM per device.

v0:
```python
import jax
import jax.numpy as jnp
from jax import lax
from jax.sharding import PartitionSpec as P

HEADS = 16
HD = 64
EXPERTS = 16
TOPK = 2
SINKS = 4
WIN = 4096
CAP = 8
EPSILON = 1e-06
MASKED = -1e30


def rms_scale(values, gain_row):
    widened = values.astype(jnp.float32)
    inverse = lax.rsqrt(jnp.mean(widened * widened, axis=-1, keepdims=True) + EPSILON)
    return (widened * inverse * gain_row).astype(jnp.bfloat16)


def by_heads(values, factor):
    shaped = values.reshape(factor.shape + (values.shape[-1] // factor.shape[-1],))
    return (shaped * factor[..., None]).reshape(values.shape)


def expert_tail(gate_up, down_rows, own_expert, local_experts):
    hidden = (jax.nn.gelu(gate_up[0], approximate=True) * gate_up[1]).astype(jnp.bfloat16)
    outputs = jnp.einsum("nkf,fd->nkd", hidden, down_rows, preferred_element_type=jnp.float32)
    placing = (jnp.arange(local_experts, dtype=jnp.int32) == own_expert).astype(jnp.float32)
    return outputs[:, None, :, :] * placing[None, :, None, None]


def body(
    tokens,
    attn_gain,
    w_qkv,
    window_cache,
    sink_cache,
    lengths,
    w_out,
    moe_gain,
    router,
    expert_ids,
    slot_order,
    expert_in,
    expert_down,
):
    requests, step_count, model_width = tokens.shape
    row_count = requests * step_count
    seq_index = lax.axis_index("seq")
    seq_count = lax.axis_size("seq")
    group_count = lax.axis_size("exp")
    local_experts = EXPERTS // group_count
    own_expert = seq_index // (seq_count // local_experts)
    in_rows = expert_in[:, 0]
    down_rows = expert_down[0]
    contract = (((1,), (1,)), ((), ()))
    flat_rows = tokens.reshape(row_count, model_width)
    normed_attn = rms_scale(flat_rows, attn_gain)
    local_mix = lax.dot_general(
        normed_attn, w_qkv, contract, preferred_element_type=jnp.float32
    ).astype(jnp.bfloat16)
    mixed_rows = lax.all_gather(local_mix, "seq", axis=1, tiled=True).reshape(
        requests, step_count, 3, HEADS, HD
    )
    queries = mixed_rows[:, :, 0]
    new_keys = mixed_rows[:, :, 1]
    new_values = mixed_rows[:, :, 2]
    score_scale = HD ** (-0.5)
    slot_span = window_cache.shape[2]
    slot_ids = seq_index * slot_span + jnp.arange(slot_span, dtype=jnp.int32)
    cache_keys = window_cache[0].reshape(requests, slot_span, HEADS, HD)
    cache_values = window_cache[1].reshape(requests, slot_span, HEADS, HD)
    window_scores = (
        jnp.einsum("rshe,rwhe->rshw", queries, cache_keys, preferred_element_type=jnp.float32)
        * score_scale
    )
    filled = jnp.minimum(WIN, lengths - SINKS)
    step_ids = jnp.arange(step_count, dtype=jnp.int32)
    written = (lengths[:, None] + step_ids[None, :] - SINKS) % WIN
    overwritten = (
        jnp.cumsum((slot_ids[None, None, :] == written[:, :, None]).astype(jnp.int32), axis=1) > 0
    )
    window_live = (
        (slot_ids[None, None, :] < filled[:, None, None]) & jnp.logical_not(overwritten)
    )[:, :, None, :]
    sink_keys = sink_cache[0].reshape(requests, SINKS, HEADS, HD)
    sink_values = sink_cache[1].reshape(requests, SINKS, HEADS, HD)
    local_keys = jnp.concatenate([sink_keys, new_keys], axis=1)
    local_values = jnp.concatenate([sink_values, new_values], axis=1)
    local_scores = (
        jnp.einsum("rshe,rkhe->rshk", queries, local_keys, preferred_element_type=jnp.float32)
        * score_scale
    )
    causal = jnp.concatenate(
        [jnp.ones((step_count, SINKS), jnp.bool_), step_ids[None, :] <= step_ids[:, None]], axis=1
    )
    local_live = causal[None, :, None, :] & (seq_index == 0)
    peak_score = jnp.maximum(
        jnp.max(jnp.where(window_live, window_scores, MASKED), axis=-1),
        jnp.max(jnp.where(local_live, local_scores, MASKED), axis=-1),
    )
    window_exp = jnp.where(window_live, jnp.exp(window_scores - peak_score[..., None]), 0.0)
    local_exp = jnp.where(local_live, jnp.exp(local_scores - peak_score[..., None]), 0.0)
    weight_sum = jnp.sum(window_exp, axis=-1) + jnp.sum(local_exp, axis=-1)
    weighted = jnp.einsum(
        "rshw,rwhe->rshe",
        window_exp.astype(jnp.bfloat16),
        cache_values,
        preferred_element_type=jnp.float32,
    )
    weighted = weighted + jnp.einsum(
        "rshk,rkhe->rshe",
        local_exp.astype(jnp.bfloat16),
        local_values,
        preferred_element_type=jnp.float32,
    )
    weighted = weighted.reshape(requests, step_count, model_width)
    overall = lax.pmax(peak_score, "seq")
    factor = jnp.exp(peak_score - overall)
    weight_sum, weighted = (
        lax.psum((weight_sum * factor).astype(jnp.bfloat16), "seq").astype(jnp.float32),
        lax.psum(by_heads(weighted, factor).astype(jnp.bfloat16), "seq").astype(jnp.float32),
    )
    attended = by_heads(weighted, 1.0 / weight_sum).astype(jnp.bfloat16)
    local_proj = lax.dot_general(
        attended.reshape(row_count, model_width),
        w_out,
        contract,
        preferred_element_type=jnp.float32,
    ).astype(jnp.bfloat16)
    projected = lax.all_gather(local_proj, "seq", axis=1, tiled=True)
    residual = flat_rows.astype(jnp.float32) + projected.astype(jnp.float32)
    normed_moe = rms_scale(residual, moe_gain)
    logits = jnp.dot(normed_moe, router, preferred_element_type=jnp.float32)
    chosen = expert_ids.reshape(row_count, TOPK)
    onehot = (chosen[:, :, None] == jnp.arange(EXPERTS, dtype=jnp.int32)).astype(jnp.float32)
    gate_values = jax.nn.sigmoid(jnp.sum(onehot * logits[:, None, :], axis=-1))
    priority = slot_order[0]
    earlier = (priority[None, :] < priority[:, None]).astype(jnp.float32)
    counts = jnp.dot(earlier, jnp.sum(onehot, axis=1), precision=lax.Precision.HIGHEST)
    position = jnp.sum(onehot * counts[:, None, :], axis=-1).astype(jnp.int32)
    column = chosen * CAP + position
    select = (
        (column[:, :, None] == jnp.arange(EXPERTS * CAP, dtype=jnp.int32))
        & (position < CAP)[:, :, None]
    ).astype(jnp.bfloat16)
    dispatch = jnp.sum(select, axis=1)
    buffer = lax.dot_general(
        dispatch, normed_moe, (((0,), (0,)), ((), ())), preferred_element_type=jnp.float32
    ).astype(jnp.bfloat16)
    buffer = buffer.reshape(group_count, local_experts, CAP, model_width)
    own_rows = lax.dynamic_index_in_dim(
        lax.all_to_all(buffer, "exp", split_axis=0, concat_axis=0, tiled=True),
        own_expert,
        1,
        keepdims=False,
    )
    gate_up = jnp.einsum("nkd,pfd->pnkf", own_rows, in_rows, preferred_element_type=jnp.float32)
    expert_part = expert_tail(gate_up, down_rows, own_expert, local_experts)
    summed = lax.psum(expert_part.astype(jnp.bfloat16), "seq")
    returned = lax.all_to_all(summed, "exp", split_axis=0, concat_axis=0, tiled=True).reshape(
        EXPERTS * CAP, model_width
    )
    picked = jnp.einsum("rkc,cd->rkd", select, returned, preferred_element_type=jnp.float32)
    final_rows = (residual + jnp.sum(gate_values[:, :, None] * picked, axis=1)).astype(jnp.bfloat16)
    result = final_rows.reshape(requests, step_count, model_width)
    return result


def solution(mesh):
    in_specs = (
        P("exp", None, None),
        P(),
        P("seq", None),
        P(None, "exp", "seq", None),
        P(None, "exp", None, None),
        P("exp"),
        P("seq", None),
        P(),
        P(),
        P("exp", None, None),
        P("exp", None),
        P(None, "exp", "seq", None),
        P("exp", "seq", None),
    )
    out_specs = P("exp", None, None)
    return jax.shard_map(body, mesh=mesh, in_specs=in_specs, out_specs=out_specs, check_vma=False)
```

profile of v0, /device:TPU:2, one launch (start us, length us, event | category | flops | bytes accessed | tf_op | source)
XLA Modules:
  0.0 496.3 jit_solution(1817082701008093470)
XLA Ops:
  6.5 0.8 add_select_fusion
  7.3 0.7 add_minimum_fusion
  8.0 0.9 reshape.165
  8.9 1.0 multiply_reduce_fusion.1
  10.2 6.6 %fusion.66 = (bf16[1,12,128,1024]{3,2,1,0:T(8,128)(2,1)}, bf16[1,12,128,1024]{3,2,1,0:T(8,128)(2,1)}) fusion(bf16[2,12,128,1024]{3,2,1,0:T(8,128)(2,1)} %param.16), kind=kLoop, calls=%fused_computation.111 | loop fusion | bytes 12582912 | tf_op jit(solution)/shard_map/slice | solution.py:75
  16.8 4.8 copy.86
  21.9 24.9 %all-gather = bf16[32,96,48]{1,2,0:T(8,128)(2,1)S(1)} all-gather(bf16[1,96,48]{1,2,0:T(8,128)(2,1)S(1)} %fusion.6), channel_id=1, replica_groups=mesh['seq'=32,'exp'=8] {'seq'}, dimensions={0}, use_global_device_ids=true | all-gather | bytes 304128 | tf_op jit(solution)/shard_map/all_gather | solution.py:65
  46.9 0.5 reshape.167
  47.4 0.4 reshape.160
  48.0 2.9 select_reduce_fusion.1
  51.6 0.5 select_reduce_fusion
  52.4 109.0 %pmax.7 = f32[12,4,16]{2,1,0:T(4,128)S(1)} all-reduce(f32[12,4,16]{2,1,0:T(4,128)S(1)} %max.9), channel_id=1, replica_groups=mesh['seq'=32,'exp'=8] {'seq'}, use_global_device_ids=true, to_apply=%region_4.5 | all-reduce | flops 768 | bytes 6144 | tf_op jit(solution)/shard_map/pmax | solution.py:121
  161.4 0.5 fusion.16
  162.0 0.5 fusion.18
  163.1 4.7 copy.92
  168.0 0.5 convolution_bitcast_fusion
  168.5 3.7 fusion.4
  172.3 0.8 convert_element_type.106
  173.1 123.8 %psum.22 = bf16[12,4,16]{2,1,0:T(4,128)(2,1)S(1)} all-reduce(bf16[12,4,16]{2,1,0:T(4,128)(2,1)S(1)} %get-tuple-element.7), channel_id=1, replica_groups=mesh['seq'=32,'exp'=8] {'seq'}, use_global_device_ids=true, to_apply=%region_8.9 | all-reduce | flops 768 | bytes 3072 | tf_op jit(solution)/shard_map/psum | solution.py:124
  297.8 0.6 all-reduce.4.cloned.1.call-done
  298.4 0.9 multiply_convert_fusion.2
  299.5 39.6 %all_gather.7 = bf16[48,1024]{0,1:T(8,128)(2,1)S(1)} all-gather(bf16[48,32]{0,1:T(8,128)(2,1)S(1)} %convolution_convert_fusion.2), channel_id=1, replica_groups=mesh['seq'=32,'exp'=8] {'seq'}, dimensions={1}, use_global_device_ids=true | all-gather | bytes 101376 | tf_op jit(solution)/shard_map/all_gather | solution.py:134
  339.8 1.0 convolution_convert_fusion
  340.8 8.5 %all-to-all-start = ((bf16[8,2,8,1024]{3,2,1,0:T(8,128)(2,1)}), bf16[8,2,8,1024]{3,2,1,0:T(8,128)(2,1)S(1)}, u32[]{:S(2)}, u32[]{:S(2)}) async-start(bf16[8,2,8,1024]{3,2,1,0:T(8,128)(2,1)} %bitcast.13), calls=%async_computation | async-start | bytes 524288 | tf_op jit(solution)/shard_map/all_to_all | solution.py:156
  349.3 12.3 %all-to-all-done = bf16[8,2,8,1024]{3,2,1,0:T(8,128)(2,1)S(1)} async-done(((bf16[8,2,8,1024]{3,2,1,0:T(8,128)(2,1)}), bf16[8,2,8,1024]{3,2,1,0:T(8,128)(2,1)S(1)}, u32[]{:S(2)}, u32[]{:S(2)}) %all-to-all-start) | async-done | bytes 262176 | tf_op jit(solution)/shard_map/all_to_all | solution.py:156
  361.7 0.4 convolution_bitcast_fusion.2
  362.2 0.8 multiply_convert_fusion
  363.1 106.3 %all-reduce.6.cloned.1.call-done = bf16[8,2,8,1024]{3,2,1,0:T(8,128)(2,1)} async-done(((bf16[8,2,8,1024]{3,2,1,0:T(8,128)(2,1)}), bf16[8,2,8,1024]{3,2,1,0:T(8,128)(2,1)}) %all-reduce.6.cloned.1.call-update) | async-done | bytes 262160 | tf_op jit(solution)/shard_map/psum | solution.py:163
  469.3 7.0 %all-to-all-start.1 = ((bf16[8,2,8,1024]{3,2,1,0:T(8,128)(2,1)}), bf16[8,2,8,1024]{3,2,1,0:T(8,128)(2,1)S(1)}, u32[]{:S(2)}, u32[]{:S(2)}) async-start(bf16[8,2,8,1024]{3,2,1,0:T(8,128)(2,1)} %all-reduce.6.cloned.1.call-done), calls=%async_computation.1 | async-start | bytes 524288 | tf_op jit(solution)/shard_map/all_to_all | solution.py:164
  476.3 12.2 %all-to-all-done.1 = bf16[8,2,8,1024]{3,2,1,0:T(8,128)(2,1)S(1)} async-done(((bf16[8,2,8,1024]{3,2,1,0:T(8,128)(2,1)}), bf16[8,2,8,1024]{3,2,1,0:T(8,128)(2,1)S(1)}, u32[]{:S(2)}, u32[]{:S(2)}) %all-to-all-start.1) | async-done | bytes 262176 | tf_op jit(solution)/shard_map/all_to_all | solution.py:164
  488.5 0.3 fusion.5
  488.8 0.7 reshape.164
  (74 shorter events, 4.5 us)
Async XLA Ops:
  6.5 355.1 %copy-start = (bf16[2,1,176,1024]{3,2,1,0:T(8,128)(2,1)S(1)}, bf16[2,1,176,1024]{3,2,1,0:T(8,128)(2,1)}, u32[]{:S(2)}) copy-start(bf16[2,1,176,1024]{3,2,1,0:T(8,128)(2,1)} %param.24) | copy-start | bytes 2162692
  6.5 291.9 %all-reduce.4.cloned.1.call-start = ((), (), s32[]{:S(2)}) async-start(), calls=%async_computation.2 | async-start | bytes 196608 | tf_op jit(solution)/shard_map/psum | solution.py:125
  16.8 4.9 copy-start.2
  16.8 4.9 copy-start.6
  47.4 3.7 copy-start.3
  168.5 128.5 %copy-start.8 = (s32[12,4,2]{0,2,1:T(2,128)S(1)}, s32[12,4,2]{0,2,1:T(2,128)}, u32[]{:S(2)}) copy-start(s32[12,4,2]{0,2,1:T(2,128)} %param.22) | copy-start | bytes 1156
  168.5 128.7 %copy-start.9 = (s32[1,48]{1,0:T(1,128)S(1)}, s32[1,48]{1,0:T(1,128)}, u32[]{:S(2)}) copy-start(s32[1,48]{1,0:T(1,128)} %param.23) | copy-start | bytes 580
  168.5 130.9 %copy-start.4 = (bf16[32,1024]{1,0:T(8,128)(2,1)S(1)}, bf16[32,1024]{1,0:T(8,128)(2,1)}, u32[]{:S(2)}) copy-start(bf16[32,1024]{1,0:T(8,128)(2,1)} %param.19) | copy-start | bytes 196612
  168.5 170.9 %copy-start.7 = (f32[1024]{0:T(1024)S(1)}, f32[1024]{0:T(1024)}, u32[]{:S(2)}) copy-start(f32[1024]{0:T(1024)} %param.20) | copy-start | bytes 12292
  172.3 167.3 %copy-start.5 = (bf16[1024,16]{0,1:T(8,128)(2,1)S(1)}, bf16[1024,16]{0,1:T(8,128)(2,1)}, u32[]{:S(2)}) copy-start(bf16[1024,16]{0,1:T(8,128)(2,1)} %param.21) | copy-start | bytes 98308
  172.3 189.8 %copy-start.1 = (bf16[1,176,1024]{2,1,0:T(8,128)(2,1)S(1)}, bf16[1,176,1024]{2,1,0:T(8,128)(2,1)}, u32[]{:S(2)}) copy-start(bf16[1,176,1024]{2,1,0:T(8,128)(2,1)} %param.25) | copy-start | bytes 1081348
  340.8 20.9 %all-to-all-start = ((bf16[8,2,8,1024]{3,2,1,0:T(8,128)(2,1)}), bf16[8,2,8,1024]{3,2,1,0:T(8,128)(2,1)S(1)}, u32[]{:S(2)}, u32[]{:S(2)}) async-start(bf16[8,2,8,1024]{3,2,1,0:T(8,128)(2,1)} %bitcast.13), calls=%async_computation | async-start | bytes 524288 | tf_op jit(solution)/shard_map/all_to_all | solution.py:156
  349.3 120.1 %all-reduce.6.cloned.1.call-start = ((), (), s32[]{:S(2)}) async-start(), calls=%async_computation.3 | async-start | bytes 524288 | tf_op jit(solution)/shard_map/psum | solution.py:163
  469.3 19.2 %all-to-all-start.1 = ((bf16[8,2,8,1024]{3,2,1,0:T(8,128)(2,1)}), bf16[8,2,8,1024]{3,2,1,0:T(8,128)(2,1)S(1)}, u32[]{:S(2)}, u32[]{:S(2)}) async-start(bf16[8,2,8,1024]{3,2,1,0:T(8,128)(2,1)} %all-reduce.6.cloned.1.call-done), calls=%async_computation.1 | async-start | bytes 524288 | tf_op jit(solution)/shard_map/all_to_all | solution.py:164
Sparse Core Ops, SparseCore 0:
  173.3 125.0 all-reduce.3
  363.2 106.0 all-reduce.5
where the time goes:
time: 497 us; the launch traced here: 496 us
  blocking collectives  297 us (60%)
  waiting for transfers between devices  131 us (26%)
  local copies, waits for them, and re-layouts  22.1 us (4%)
  starting transfers between devices  15.5 us (3%)
  between operations  13.8 us (3%)
  matrix products  10.1 us (2%)
  other arithmetic  6.1 us (1%)
    psum x1, blocking collectives, body(): lax.psum((weight_sum * factor).astype(jnp.bfloat16), 'seq')  124 us
    pmax x1, blocking collectives, body(): overall = lax.pmax(peak_score, 'seq')  109 us
    psum x1, waiting for transfers between devices, body(): summed = lax.psum(expert_part.astype(jnp.bfloat16), 'seq')  106 us
    all_gather x1, blocking collectives, body(): projected = lax.all_gather(local_proj, 'seq', axis=1, tiled=True)  39.6 us
    all_gather x1, blocking collectives, body(): lax.all_gather(local_mix, 'seq', axis=1, tiled=True)  24.9 us
    all_to_all x1, waiting for transfers between devices, body(): lax.all_to_all(buffer, 'exp', split_axis=0, concat_axis=0, tiled=True)  12.3 us
    all_to_all x1, waiting for transfers between devices, body(): lax.all_to_all(summed, 'exp', split_axis=0, concat_axis=0, tiled=True)  12.2 us
    slice x2, local copies, waits for them, and re-layouts, body(): cache_values = window_cache[1].reshape(requests, slot_span, HEADS, HD)  11.3 us
  transfers between devices with their start and end apart: 4, of which 4 were waited for; matrix products, arithmetic and copies ran while one was open for 0% of the time, Pallas kernels for 0%

commit v1 on v0

--- a/solution.py
+++ b/solution.py
@@ -131,7 +131,9 @@
         contract,
         preferred_element_type=jnp.float32,
     ).astype(jnp.bfloat16)
-    projected = lax.all_gather(local_proj, "seq", axis=1, tiled=True)
+    projected = jnp.concatenate(
+        lax.all_to_all(jnp.stack([local_proj] * lax.psum(1, "seq")), "seq", 0, 0), axis=1
+    )
     residual = flat_rows.astype(jnp.float32) + projected.astype(jnp.float32)
     normed_moe = rms_scale(residual, moe_gain)
     logits = jnp.dot(normed_moe, router, preferred_element_type=jnp.float32)

time: 497 us -> 487 us (0.980)
  blocking collectives: 297 us -> 258 us
  starting transfers between devices: 15.5 us -> 36.7 us
  waiting for transfers between devices: 131 us -> 137 us
    all_gather x1 -> x0, blocking collectives: 39.6 us -> none  [body(): projected = lax.all_gather(local_proj, 'seq', axis=1, tiled=True)]
    all_to_all x0 -> x1, starting transfers between devices: none -> 21.2 us  [body(): lax.all_to_all(jnp.stack([local_proj] * lax.psum(1, 'seq')), 'seq', 0, 0)]
    all_to_all x0 -> x1, waiting for transfers between devices: none -> 6.28 us  [body(): lax.all_to_all(jnp.stack([local_proj] * lax.psum(1, 'seq')), 'seq', 0, 0)]
  transfers between devices with their start and end apart: 4 -> 5, of which waited for: 4 -> 5; matrix products, arithmetic and copies ran while one was open for 0% -> 0% of each run, Pallas kernels for 0% -> 0%
where the time goes in v1:
time: 487 us; the launch traced here: 486 us
  blocking collectives  258 us (53%)
  waiting for transfers between devices  137 us (28%)
  starting transfers between devices  36.7 us (8%)
  local copies, waits for them, and re-layouts  24 us (5%)
  between operations  13.9 us (3%)
  matrix products  10.1 us (2%)
  other arithmetic  6.9 us (1%)
    psum x1, blocking collectives, body(): lax.psum((weight_sum * factor).astype(jnp.bfloat16), 'seq')  124 us
    pmax x1, blocking collectives, body(): overall = lax.pmax(peak_score, 'seq')  109 us
    psum x1, waiting for transfers between devices, body(): summed = lax.psum(expert_part.astype(jnp.bfloat16), 'seq')  105 us
    all_gather x1, blocking collectives, body(): lax.all_gather(local_mix, 'seq', axis=1, tiled=True)  24.9 us
    all_to_all x1, starting transfers between devices, body(): lax.all_to_all(jnp.stack([local_proj] * lax.psum(1, 'seq')), 'seq', 0, 0)  21.2 us
    all_to_all x1, waiting for transfers between devices, body(): lax.all_to_all(summed, 'exp', split_axis=0, concat_axis=0, tiled=True)  12.2 us
    all_to_all x1, waiting for transfers between devices, body(): lax.all_to_all(buffer, 'exp', split_axis=0, concat_axis=0, tiled=True)  12.1 us
    slice x2, local copies, waits for them, and re-layouts, body(): cache_values = window_cache[1].reshape(requests, slot_span, HEADS, HD)  11.3 us
  transfers between devices with their start and end apart: 5, of which 5 were waited for; matrix products, arithmetic and copies ran while one was open for 0% of the time, Pallas kernels for 0%

profile of v1, /device:TPU:2, one launch (start us, length us, event | category | flops | bytes accessed | tf_op | source)
XLA Modules:
  0.0 486.0 jit_solution(486405315053313673)
XLA Ops:
  6.5 0.8 add_select_fusion
  7.3 0.7 add_minimum_fusion
  8.0 0.9 reshape.182
  8.9 1.0 multiply_reduce_fusion.1
  10.2 6.6 %fusion.66 = (bf16[1,12,128,1024]{3,2,1,0:T(8,128)(2,1)}, bf16[1,12,128,1024]{3,2,1,0:T(8,128)(2,1)}) fusion(bf16[2,12,128,1024]{3,2,1,0:T(8,128)(2,1)} %param.16), kind=kLoop, calls=%fused_computation.112 | loop fusion | bytes 12582912 | tf_op jit(solution)/shard_map/slice | solution.py:75
  16.8 4.8 copy.83
  21.9 24.9 %all-gather = bf16[32,96,48]{1,2,0:T(8,128)(2,1)S(1)} all-gather(bf16[1,96,48]{1,2,0:T(8,128)(2,1)S(1)} %fusion.6), channel_id=1, replica_groups=mesh['seq'=32,'exp'=8] {'seq'}, dimensions={0}, use_global_device_ids=true | all-gather | bytes 304128 | tf_op jit(solution)/shard_map/all_gather | solution.py:65
  46.9 0.5 reshape.186
  48.0 2.9 select_reduce_fusion.1
  51.6 0.5 select_reduce_fusion
  52.4 109.0 %pmax.7 = f32[12,4,16]{2,1,0:T(4,128)S(1)} all-reduce(f32[12,4,16]{2,1,0:T(4,128)S(1)} %max.9), channel_id=1, replica_groups=mesh['seq'=32,'exp'=8] {'seq'}, use_global_device_ids=true, to_apply=%region_4.5 | all-reduce | flops 768 | bytes 6144 | tf_op jit(solution)/shard_map/pmax | solution.py:121
  161.4 0.5 fusion.16
  162.0 0.5 fusion.18
  163.1 4.7 copy.89
  168.0 0.5 convolution_bitcast_fusion
  168.5 3.7 fusion.4
  172.3 0.8 convert_element_type.123
  173.1 123.8 %psum.22 = bf16[12,4,16]{2,1,0:T(4,128)(2,1)S(1)} all-reduce(bf16[12,4,16]{2,1,0:T(4,128)(2,1)S(1)} %get-tuple-element.7), channel_id=1, replica_groups=mesh['seq'=32,'exp'=8] {'seq'}, use_global_device_ids=true, to_apply=%region_8.9 | all-reduce | flops 768 | bytes 3072 | tf_op jit(solution)/shard_map/psum | solution.py:124
  297.6 0.8 all-reduce.4.cloned.1.call-done
  298.4 0.9 multiply_convert_fusion.2
  299.6 1.0 reshape.191
  300.6 21.2 %all-to-all-start = ((bf16[32,2,768]{2,1,0:T(2,128)(2,1)}), bf16[32,2,768]{2,1,0:T(2,128)(2,1)S(1)}, u32[]{:S(2)}, u32[]{:S(2)}) async-start(bf16[32,2,768]{2,1,0:T(2,128)(2,1)} %reshape.191), calls=%async_computation | async-start | bytes 196608 | tf_op jit(solution)/shard_map/all_to_all | solution.py:135
  322.0 6.3 %all-to-all-done = bf16[32,2,768]{2,1,0:T(2,128)(2,1)S(1)} async-done(((bf16[32,2,768]{2,1,0:T(2,128)(2,1)}), bf16[32,2,768]{2,1,0:T(2,128)(2,1)S(1)}, u32[]{:S(2)}, u32[]{:S(2)}) %all-to-all-start) | async-done | bytes 98336 | tf_op jit(solution)/shard_map/all_to_all | solution.py:135
  328.8 0.7 copy.97
  330.6 1.0 convolution_convert_fusion
  331.6 8.5 %all-to-all-start.1 = ((bf16[8,2,8,1024]{3,2,1,0:T(8,128)(2,1)}), bf16[8,2,8,1024]{3,2,1,0:T(8,128)(2,1)S(1)}, u32[]{:S(2)}, u32[]{:S(2)}) async-start(bf16[8,2,8,1024]{3,2,1,0:T(8,128)(2,1)} %bitcast.15), calls=%async_computation.1 | async-start | bytes 524288 | tf_op jit(solution)/shard_map/all_to_all | solution.py:158
  340.1 12.1 %all-to-all-done.1 = bf16[8,2,8,1024]{3,2,1,0:T(8,128)(2,1)S(1)} async-done(((bf16[8,2,8,1024]{3,2,1,0:T(8,128)(2,1)}), bf16[8,2,8,1024]{3,2,1,0:T(8,128)(2,1)S(1)}, u32[]{:S(2)}, u32[]{:S(2)}) %all-to-all-start.1) | async-done | bytes 262176 | tf_op jit(solution)/shard_map/all_to_all | solution.py:158
  352.8 0.8 multiply_convert_fusion
  353.6 105.3 %all-reduce.6.cloned.1.call-done = bf16[8,2,8,1024]{3,2,1,0:T(8,128)(2,1)} async-done(((bf16[8,2,8,1024]{3,2,1,0:T(8,128)(2,1)}), bf16[8,2,8,1024]{3,2,1,0:T(8,128)(2,1)}) %all-reduce.6.cloned.1.call-update) | async-done | bytes 262160 | tf_op jit(solution)/shard_map/psum | solution.py:165
  458.9 7.0 %all-to-all-start.2 = ((bf16[8,2,8,1024]{3,2,1,0:T(8,128)(2,1)}), bf16[8,2,8,1024]{3,2,1,0:T(8,128)(2,1)S(1)}, u32[]{:S(2)}, u32[]{:S(2)}) async-start(bf16[8,2,8,1024]{3,2,1,0:T(8,128)(2,1)} %all-reduce.6.cloned.1.call-done), calls=%async_computation.2 | async-start | bytes 524288 | tf_op jit(solution)/shard_map/all_to_all | solution.py:166
  465.9 12.2 %all-to-all-done.2 = bf16[8,2,8,1024]{3,2,1,0:T(8,128)(2,1)S(1)} async-done(((bf16[8,2,8,1024]{3,2,1,0:T(8,128)(2,1)}), bf16[8,2,8,1024]{3,2,1,0:T(8,128)(2,1)S(1)}, u32[]{:S(2)}, u32[]{:S(2)}) %all-to-all-start.2) | async-done | bytes 262176 | tf_op jit(solution)/shard_map/all_to_all | solution.py:166
  478.4 0.7 add_convert_fusion
  (85 shorter events, 6.4 us)
Async XLA Ops:
  6.5 345.7 %copy-start = (bf16[2,1,176,1024]{3,2,1,0:T(8,128)(2,1)S(1)}, bf16[2,1,176,1024]{3,2,1,0:T(8,128)(2,1)}, u32[]{:S(2)}) copy-start(bf16[2,1,176,1024]{3,2,1,0:T(8,128)(2,1)} %param.24) | copy-start | bytes 2162692
  6.5 291.9 %all-reduce.4.cloned.1.call-start = ((), (), s32[]{:S(2)}) async-start(), calls=%async_computation.3 | async-start | bytes 196608 | tf_op jit(solution)/shard_map/psum | solution.py:125
  16.8 4.9 %copy-start.3 = (bf16[96,1024]{1,0:T(8,128)(2,1)S(1)}, bf16[96,1024]{1,0:T(8,128)(2,1)}, u32[]{:S(2)}) copy-start(bf16[96,1024]{1,0:T(8,128)(2,1)} %param.15) | copy-start | bytes 589828
  16.8 4.9 %copy-start.7 = (f32[1024]{0:T(1024)S(1)}, f32[1024]{0:T(1024)}, u32[]{:S(2)}) copy-start(f32[1024]{0:T(1024)} %param.14) | copy-start | bytes 12292
  47.4 3.7 copy-start.4
  168.5 128.5 %copy-start.9 = (s32[12,4,2]{0,2,1:T(2,128)S(1)}, s32[12,4,2]{0,2,1:T(2,128)}, u32[]{:S(2)}) copy-start(s32[12,4,2]{0,2,1:T(2,128)} %param.22) | copy-start | bytes 1156
  168.5 130.9 %copy-start.5 = (bf16[32,1024]{1,0:T(8,128)(2,1)S(1)}, bf16[32,1024]{1,0:T(8,128)(2,1)}, u32[]{:S(2)}) copy-start(bf16[32,1024]{1,0:T(8,128)(2,1)} %param.19) | copy-start | bytes 196612
  168.5 153.3 %copy-start.10 = (s32[1,48]{1,0:T(1,128)S(1)}, s32[1,48]{1,0:T(1,128)}, u32[]{:S(2)}) copy-start(s32[1,48]{1,0:T(1,128)} %param.23) | copy-start | bytes 580
  299.3 30.6 %copy-start.1 = (bf16[12,4,1024]{2,1,0:T(4,128)(2,1)S(1)}, bf16[12,4,1024]{2,1,0:T(4,128)(2,1)}, u32[]{:S(2)}) copy-start(bf16[12,4,1024]{2,1,0:T(4,128)(2,1)} %param.13) | copy-start | bytes 294916
  299.4 30.8 %copy-start.8 = (f32[1024]{0:T(1024)S(1)}, f32[1024]{0:T(1024)}, u32[]{:S(2)}) copy-start(f32[1024]{0:T(1024)} %param.20) | copy-start | bytes 12292
  299.6 30.7 %copy-start.6 = (bf16[1024,16]{0,1:T(8,128)(2,1)S(1)}, bf16[1024,16]{0,1:T(8,128)(2,1)}, u32[]{:S(2)}) copy-start(bf16[1024,16]{0,1:T(8,128)(2,1)} %param.21) | copy-start | bytes 98308
  300.6 27.6 %all-to-all-start = ((bf16[32,2,768]{2,1,0:T(2,128)(2,1)}), bf16[32,2,768]{2,1,0:T(2,128)(2,1)S(1)}, u32[]{:S(2)}, u32[]{:S(2)}) async-start(bf16[32,2,768]{2,1,0:T(2,128)(2,1)} %reshape.191), calls=%async_computation | async-start | bytes 196608 | tf_op jit(solution)/shard_map/all_to_all | solution.py:135
  328.6 23.9 %copy-start.2 = (bf16[1,176,1024]{2,1,0:T(8,128)(2,1)S(1)}, bf16[1,176,1024]{2,1,0:T(8,128)(2,1)}, u32[]{:S(2)}) copy-start(bf16[1,176,1024]{2,1,0:T(8,128)(2,1)} %param.25) | copy-start | bytes 1081348
  331.6 20.6 %all-to-all-start.1 = ((bf16[8,2,8,1024]{3,2,1,0:T(8,128)(2,1)}), bf16[8,2,8,1024]{3,2,1,0:T(8,128)(2,1)S(1)}, u32[]{:S(2)}, u32[]{:S(2)}) async-start(bf16[8,2,8,1024]{3,2,1,0:T(8,128)(2,1)} %bitcast.15), calls=%async_computation.1 | async-start | bytes 524288 | tf_op jit(solution)/shard_map/all_to_all | solution.py:158
  340.0 118.9 %all-reduce.6.cloned.1.call-start = ((), (), s32[]{:S(2)}) async-start(), calls=%async_computation.4 | async-start | bytes 524288 | tf_op jit(solution)/shard_map/psum | solution.py:165
  458.9 19.2 %all-to-all-start.2 = ((bf16[8,2,8,1024]{3,2,1,0:T(8,128)(2,1)}), bf16[8,2,8,1024]{3,2,1,0:T(8,128)(2,1)S(1)}, u32[]{:S(2)}, u32[]{:S(2)}) async-start(bf16[8,2,8,1024]{3,2,1,0:T(8,128)(2,1)} %all-reduce.6.cloned.1.call-done), calls=%async_computation.2 | async-start | bytes 524288 | tf_op jit(solution)/shard_map/all_to_all | solution.py:166
Sparse Core Ops, SparseCore 0:
  173.3 125.0 all-reduce.3
  353.7 105.1 all-reduce.5
